TPU v7x, 256 devices: a whole 4x4x8 slice. The times are simulated.
256 devices in a mesh: src: 32 (over x, z_lo, core), snk: 4 (over y), mom: 2 (over z_hi).
Axes of the slice: x: 4, y: 4, z: 8 (z_hi: 2, z_lo: 4; z = z_hi * 4 + z_lo), core: 2. Of those that a mesh axis runs over, the one named last changes fastest.
Arguments:
- peramb: bfloat16 [96, 16, 256, 256], P(None, 'snk', 'src'), may hold values from -0.375 to 0.375
- elem_src: bfloat16 [96, 16, 256, 256], P('src', 'mom'), may hold values from -6 to 6
- elem_snk: bfloat16 [96, 16, 256, 256], P('src', 'mom'), may hold values from -6 to 6
- op_elem: int32 [64], replicated, may hold values from 0 to 15
- hlt_kernel: float32 [16, 128], replicated, may hold values from -1.5 to 1.5
Outputs:
- smeared: float32 [64, 16, 128], P('src', 'mom')
All inputs are finite; a program needn't handle non-finite values.
Results may differ from a plain program's by a relative error of at most 0.004.
Values may be sent and summed in bfloat16 or wider, within the bound.
A program may use at most 128 MiB of HBM per device.

v0:
```python
import math

import jax
import jax.numpy as jnp
from jax import lax
from jax.sharding import PartitionSpec as P


def shifted(value, axis, steps):
    count = lax.axis_size(axis)
    pairs = [(source, (source + steps) % count) for source in range(count)]
    return lax.ppermute(value, axis, pairs)


def body(peramb, elem_src, elem_snk, op_elem, hlt_kernel):
    source_count = peramb.shape[0]
    eigen_count = peramb.shape[3]
    highest = lax.Precision.HIGHEST
    regrouped = lax.all_to_all(peramb, "src", split_axis=0, concat_axis=2, tiled=True)
    half_product = jnp.einsum(
        "rsab,rfbc->rsfac", regrouped, elem_src, preferred_element_type=jnp.float32
    ).astype(jnp.bfloat16)
    sandwich = jnp.einsum(
        "rsfac,rsdc->rsfad", half_product, regrouped, preferred_element_type=jnp.float32
    ).astype(jnp.bfloat16)
    own_count = elem_snk.shape[0]
    sep_local = regrouped.shape[1]
    sep_total = sep_local * lax.axis_size("snk")
    reach_blocks = (own_count + sep_total - 2) // own_count
    blocks = [elem_snk] + [
        shifted(elem_snk, "src", -offset) for offset in range(1, reach_blocks + 1)
    ]
    stacked = jnp.concatenate(blocks, axis=0)
    window = lax.dynamic_slice_in_dim(
        stacked, lax.axis_index("snk") * sep_local, own_count + sep_local - 1, 0
    )
    block_elems = lax.all_gather(window, "mom", axis=1, tiled=True)
    trace_rows = [
        jnp.einsum(
            "seab,sfab->sef",
            block_elems[source_row : source_row + sep_local],
            sandwich[source_row],
            preferred_element_type=jnp.float32,
        )
        for source_row in range(own_count)
    ]
    pair_traces = jnp.stack(trace_rows, axis=0)
    elem_count = pair_traces.shape[2]
    onehot = (op_elem[:, None] == jnp.arange(elem_count, dtype=jnp.int32)[None, :]).astype(
        jnp.float32
    )
    norm_factor = 1.0 / (eigen_count * math.sqrt(source_count))
    correlator = jnp.einsum("oe,rsef->osf", onehot, pair_traces, precision=highest) * norm_factor
    owned_part = lax.psum_scatter(correlator, "src", scatter_dimension=0, tiled=True)
    all_sinks = lax.all_gather(owned_part, "snk", axis=1, tiled=True)
    result = jnp.einsum("otf,tk->ofk", all_sinks, hlt_kernel, precision=highest)
    return result


def solution(mesh):
    placed = (
        P(None, "snk", "src", None),
        P("src", "mom", None, None),
        P("src", "mom", None, None),
        P(),
        P(),
    )
    return jax.shard_map(
        body, mesh=mesh, in_specs=placed, out_specs=P("src", "mom", None), check_vma=False
    )
```

profile of v0, /device:TPU:1, one launch (start us, length us, event | category | flops | bytes accessed | tf_op | source)
XLA Modules:
  0.0 991.7 jit_solution(1708704320264747332)
XLA Ops:
  6.5 0.0 copy-start
  6.5 0.0 all-gather.2.cloned.1.call-start
  6.5 3.2 collective-permute-start
  9.8 4.8 collective-permute-start.1
  14.6 0.0 collective-permute-start.2
  14.6 2.8 collective-permute-start.3
  17.4 0.3 collective-permute-start.4
  17.7 3.9 constant_dynamic-update-slice_fusion.5
  21.5 55.6 %collective-permute-done = bf16[3,8,256,256]{3,2,1,0:T(8,128)(2,1)} collective-permute-done((bf16[3,8,256,256]{3,2,1,0:T(8,128)(2,1)}, bf16[3,8,256,256]{3,2,1,0:T(8,128)(2,1)}, u32[]{:S(2)}, u32[]{:S(2)}) %collective-permute-start) | collective-permute-done | bytes 3145760 | tf_op jit(solution)/shard_map/ppermute | solution.py:12
  77.1 3.9 constant_dynamic-update-slice_fusion.4
  81.0 1.9 collective-permute-done.1
  82.9 3.9 constant_dynamic-update-slice_fusion.3
  86.8 296.7 %collective-permute-done.2 = bf16[3,8,256,256]{3,2,1,0:T(8,128)(2,1)} collective-permute-done((bf16[3,8,256,256]{3,2,1,0:T(8,128)(2,1)}, bf16[3,8,256,256]{3,2,1,0:T(8,128)(2,1)}, u32[]{:S(2)}, u32[]{:S(2)}) %collective-permute-start.2) | collective-permute-done | bytes 3145760 | tf_op jit(solution)/shard_map/ppermute | solution.py:12
  383.5 3.9 constant_dynamic-update-slice_fusion.2
  387.4 0.0 collective-permute-done.3
  387.4 3.8 constant_dynamic-update-slice_fusion.1
  391.2 0.0 collective-permute-done.4
  391.2 3.8 constant_dynamic-update-slice_fusion
  395.1 6.2 constant_dynamic-slice_fusion.1
  401.3 0.0 copy-start.6
  401.3 0.0 all-gather.2.cloned.1.call-update
  401.3 69.1 %all-to-all-start = ((bf16[96,4,8,256]{3,2,1,0:T(8,128)(2,1)}), bf16[96,4,8,256]{3,2,1,0:T(8,128)(2,1)}, u32[]{:S(2)}, u32[]{:S(2)}) async-start(bf16[96,4,8,256]{3,2,1,0:T(8,128)(2,1)} %param.5), calls=%async_computation | async-start | bytes 3145728 | tf_op jit(solution)/shard_map/all_to_all | solution.py:19
  470.4 0.0 copy-done.6
  470.4 0.6 dynamic-slice
  471.6 307.3 %all-to-all-done = bf16[96,4,8,256]{3,2,1,0:T(8,128)(2,1)} async-done(((bf16[96,4,8,256]{3,2,1,0:T(8,128)(2,1)}), bf16[96,4,8,256]{3,2,1,0:T(8,128)(2,1)}, u32[]{:S(2)}, u32[]{:S(2)}) %all-to-all-start) | async-done | bytes 1572896 | tf_op jit(solution)/shard_map/all_to_all | solution.py:19
  779.0 0.0 copy-done
  779.0 11.3 %fusion.11 = bf16[3,4,8,256,256]{4,3,2,1,0:T(8,128)(2,1)} fusion(bf16[3,8,256,256]{3,2,1,0:T(8,128)(2,1)S(1)} %copy-done, bf16[32,3,4,8,256]{4,3,2,1,0:T(8,128)(2,1)} %bitcast.3), kind=kOutput, calls=%fused_computation.10 | convolution fusion | flops 6455033856 | bytes 17301504 | tf_op jit(solution)/shard_map/rsfac,rsdc->rsfad/dot_general | solution.py:23
  790.3 8.9 slice_bitcast_fusion
  799.2 0.0 all-gather.2.cloned.1.call-done
  799.2 0.0 copy-start.3
  799.2 16.6 %fusion.55 = (bf16[4,16,256,256]{3,2,1,0:T(8,128)(2,1)S(1)}, bf16[4,16,256,256]{3,2,1,0:T(8,128)(2,1)}, bf16[4,16,256,256]{3,2,1,0:T(8,128)(2,1)}) fusion(bf16[6,16,256,256]{3,2,1,0:T(8,128)(2,1)} %all-gather.2.cloned.1.call-done), kind=kLoop, calls=%fused_computation.41 | loop fusion | bytes 50331648 | tf_op jit(solution)/shard_map/slice | solution.py:41
  815.8 0.0 copy-done.3
  815.8 10.0 %fusion.28 = f32[4,16,8]{2,1,0:T(8,128)S(1)} fusion(bf16[4,8,256,256]{3,2,1,0:T(8,128)(2,1)S(1)} %copy-done.3, bf16[4,16,256,256]{3,2,1,0:T(8,128)(2,1)} %get-tuple-element.6), kind=kOutput, calls=%fused_computation.21 | convolution fusion | flops 67108864 | bytes 12584960 | tf_op jit(solution)/shard_map/seab,sfab->sef/dot_general | solution.py:39
  825.8 0.0 copy-start.2
  825.8 12.1 %fusion.43 = f32[4,16,8]{2,1,0:T(8,128)S(1)} fusion(f32[4,16,8]{2,1,0:T(8,128)S(1)} %fusion.28, bf16[4,8,256,256]{3,2,1,0:T(8,128)(2,1)} %get-tuple-element.10, bf16[4,16,256,256]{3,2,1,0:T(8,128)(2,1)} %get-tuple-element.7), kind=kOutput, calls=%fused_computation.24 | convolution fusion | flops 67109376 | bytes 12587008 | tf_op jit(solution)/shard_map/seab,sfab->sef/dot_general | solution.py:39
  837.9 0.0 copy-done.2
  837.9 0.0 copy-start.5
  837.9 0.0 copy-start.4
  837.9 0.0 copy-start.1
  837.9 7.1 fusion.38
  845.0 0.0 copy-done.5
  845.0 0.2 fusion.49
  845.2 0.1 copy.21
  845.4 128.8 %all-reduce = f32[64,4,8]{2,1,0:T(4,128)S(1)} all-reduce(f32[64,4,8]{2,1,0:T(4,128)S(1)} %broadcast_multiply_fusion), channel_id=2, replica_groups=mesh['src'=32,'snk'=4,'mom'=2] {'src'}, use_global_device_ids=true, to_apply=%region_0.0.clone | all-reduce | flops 2048 | bytes 16384
  974.2 9.8 all_gather.7
  984.0 0.0 copy-done.4
  984.0 0.8 fusion.51
  984.8 0.0 copy-done.1
  (3 shorter events, 0.0 us)
Async XLA Ops:
  6.5 772.4 %copy-start = (bf16[3,8,256,256]{3,2,1,0:T(8,128)(2,1)S(1)}, bf16[3,8,256,256]{3,2,1,0:T(8,128)(2,1)}, u32[]{:S(2)}) copy-start(bf16[3,8,256,256]{3,2,1,0:T(8,128)(2,1)} %param.6) | copy-start | bytes 9437188
  6.5 792.7 %all-gather.2.cloned.1.call-start = ((), (), s32[]{:S(2)}) async-start(), calls=%async_computation.1 | async-start | bytes 18874368 | tf_op jit(solution)/shard_map/all_gather | solution.py:37
  6.5 70.6 %collective-permute-start = (bf16[3,8,256,256]{3,2,1,0:T(8,128)(2,1)}, bf16[3,8,256,256]{3,2,1,0:T(8,128)(2,1)}, u32[]{:S(2)}, u32[]{:S(2)}) collective-permute-start(bf16[3,8,256,256]{3,2,1,0:T(8,128)(2,1)} %param.7), channel_id=1, source_target_pairs={{0,248},{8,0},{16,8},{24,16},{32,24},{40,32},{48,40},{56,48},{64,5... | collective-permute-start | bytes 9437192 | tf_op jit(solution)/shard_map/ppermute | solution.py:12
  9.8 73.2 %collective-permute-start.1 = (bf16[3,8,256,256]{3,2,1,0:T(8,128)(2,1)}, bf16[3,8,256,256]{3,2,1,0:T(8,128)(2,1)}, u32[]{:S(2)}, u32[]{:S(2)}) collective-permute-start(bf16[3,8,256,256]{3,2,1,0:T(8,128)(2,1)} %param.7), channel_id=1, source_target_pairs={{0,240},{8,248},{16,0},{24,8},{32,16},{40,24},{48,32},{56,40},{64,... | collective-permute-start | bytes 9437192 | tf_op jit(solution)/shard_map/ppermute | solution.py:12
  14.6 368.9 %collective-permute-start.2 = (bf16[3,8,256,256]{3,2,1,0:T(8,128)(2,1)}, bf16[3,8,256,256]{3,2,1,0:T(8,128)(2,1)}, u32[]{:S(2)}, u32[]{:S(2)}) collective-permute-start(bf16[3,8,256,256]{3,2,1,0:T(8,128)(2,1)} %param.7), channel_id=1, source_target_pairs={{0,232},{8,240},{16,248},{24,0},{32,8},{40,16},{48,24},{56,32},{64... | collective-permute-start | bytes 9437192 | tf_op jit(solution)/shard_map/ppermute | solution.py:12
  14.6 372.8 %collective-permute-start.3 = (bf16[3,8,256,256]{3,2,1,0:T(8,128)(2,1)}, bf16[3,8,256,256]{3,2,1,0:T(8,128)(2,1)}, u32[]{:S(2)}, u32[]{:S(2)}) collective-permute-start(bf16[3,8,256,256]{3,2,1,0:T(8,128)(2,1)} %param.7), channel_id=1, source_target_pairs={{0,224},{8,232},{16,240},{24,248},{32,0},{40,8},{48,16},{56,24},{6... | collective-permute-start | bytes 9437192 | tf_op jit(solution)/shard_map/ppermute | solution.py:12
  17.4 373.9 %collective-permute-start.4 = (bf16[3,8,256,256]{3,2,1,0:T(8,128)(2,1)}, bf16[3,8,256,256]{3,2,1,0:T(8,128)(2,1)}, u32[]{:S(2)}, u32[]{:S(2)}) collective-permute-start(bf16[3,8,256,256]{3,2,1,0:T(8,128)(2,1)} %param.7), channel_id=1, source_target_pairs={{0,216},{8,224},{16,232},{24,240},{32,248},{40,0},{48,8},{56,16},{... | collective-permute-start | bytes 9437192 | tf_op jit(solution)/shard_map/ppermute | solution.py:12
  401.3 69.1 %copy-start.6 = (u32[256]{0:T(256)S(1)}, u32[256]{0:T(256)}, u32[]{:S(2)}) copy-start(u32[256]{0:T(256)} %constant.20) | copy-start | bytes 3076
  401.3 377.7 %all-to-all-start = ((bf16[96,4,8,256]{3,2,1,0:T(8,128)(2,1)}), bf16[96,4,8,256]{3,2,1,0:T(8,128)(2,1)}, u32[]{:S(2)}, u32[]{:S(2)}) async-start(bf16[96,4,8,256]{3,2,1,0:T(8,128)(2,1)} %param.5), calls=%async_computation | async-start | bytes 3145728 | tf_op jit(solution)/shard_map/all_to_all | solution.py:19
  799.2 16.6 %copy-start.3 = (bf16[4,8,256,256]{3,2,1,0:T(8,128)(2,1)S(1)}, bf16[4,8,256,256]{3,2,1,0:T(8,128)(2,1)}, u32[]{:S(2)}) copy-start(bf16[4,8,256,256]{3,2,1,0:T(8,128)(2,1)} %get-tuple-element.9) | copy-start | bytes 12582916
  825.8 12.1 %copy-start.2 = (bf16[4,8,256,256]{3,2,1,0:T(8,128)(2,1)S(1)}, bf16[4,8,256,256]{3,2,1,0:T(8,128)(2,1)}, u32[]{:S(2)}) copy-start(bf16[4,8,256,256]{3,2,1,0:T(8,128)(2,1)} %get-tuple-element.8) | copy-start | bytes 12582916
  837.9 7.2 copy-start.5
  837.9 146.1 %copy-start.4 = (f32[16,128]{1,0:T(8,128)S(1)}, f32[16,128]{1,0:T(8,128)}, u32[]{:S(2)}) copy-start(f32[16,128]{1,0:T(8,128)} %param.9) | copy-start | bytes 24580
  837.9 146.9 %copy-start.1 = (bf16[3,8,256,256]{3,2,1,0:T(8,128)(2,1)S(1)}, bf16[3,8,256,256]{3,2,1,0:T(8,128)(2,1)}, u32[]{:S(2)}) copy-start(bf16[3,8,256,256]{3,2,1,0:T(8,128)(2,1)} %param.6) | copy-start | bytes 9437188
Sparse Core Ops, SparseCore 0:
  401.4 370.2 all-gather.1
where the time goes:
time: 999 us; the launch traced here: 992 us
  waiting for transfers between devices  662 us (66%)
  blocking collectives  139 us (14%)
  starting transfers between devices  80.2 us (8%)
  local copies, waits for them, and re-layouts  55.6 us (6%)
  matrix products  41.5 us (4%)
  between operations  14.1 us (1%)
    ppermute x5, waiting for transfers between devices, shifted(): return lax.ppermute(value, axis, pairs)  354 us
    all_to_all x1, waiting for transfers between devices, body(): lax.all_to_all(peramb, 'src', split_axis=0, concat_axis=2, tiled=True)  307 us
    unnamed x1, blocking collectives  129 us
    all_to_all x1, starting transfers between devices, body(): lax.all_to_all(peramb, 'src', split_axis=0, concat_axis=2, tiled=True)  69.1 us
    dot_general x3, matrix products, body(): jnp.einsum('seab,sfab->sef', block_elems[source_row:source_row + sep_loca...  29.2 us
  transfers between devices with their start and end apart: 7, of which 4 were waited for; matrix products, arithmetic and copies ran while one was open for 4% of the time, Pallas kernels for 0%

commit v1 on v0

v1 whole, which is shorter than its diff:
```python
import functools
import math

import jax
import jax.numpy as jnp
from jax import lax
from jax.experimental import pallas as pl
from jax.experimental.pallas import tpu as pltpu
from jax.sharding import PartitionSpec as P

MESH = pl.DeviceIdType.MESH
SRC, SNK, MOM = 32, 4, 2
OWN = 3
BLOCKS = 6


def kernel(
    norm, per_ref, es_ref, ek_ref, op_ref, hlt_ref, out_ref,
    pbuf, ebuf, sbuf, hbuf, acc, part, red_a, red_b, red_c, full,
    local_sem, p_send, p_recv, e_send, e_recv, s_send, s_recv,
    py_send, py_recv, ey_send, ey_recv, r_send, r_recv,
):
    s, y, m = lax.axis_index("src"), lax.axis_index("snk"), lax.axis_index("mom")
    x, zl, core = s // 8, (s // 2) % 4, s % 2
    f32 = jnp.float32

    def near(other):
        apart = (other // 2) % 4 - zl
        return jnp.where(apart * apart == 9, 1 - m, m)

    def ids(src, snk, mom):
        return {"src": src, "snk": snk, "mom": mom}

    def remote(src, dst, send, recv, where):
        return pltpu.make_async_remote_copy(
            src_ref=src, dst_ref=dst, send_sem=send, recv_sem=recv,
            device_id=where, device_id_type=MESH,
        )

    up = ids(s, (y + 1) % SNK, m)
    down = ids(s, (y + 3) % SNK, m)
    partner = ids(s, y, 1 - m)
    onward = ids((s + SRC - 1) % SRC, y, jnp.where(s % 8 == 0, 1 - m, m))

    barrier = pltpu.get_barrier_semaphore()

    def greet(step, carry):
        other = (s + step) % SRC
        pl.semaphore_signal(barrier, inc=1, device_id=ids(other, y, near(other)), device_id_type=MESH)
        return carry

    lax.fori_loop(1, SRC, greet, 0)
    for step in range(4):
        other = x * 8 + step * 2 + core
        pl.semaphore_signal(
            barrier, inc=1, device_id=ids(other, y, 1 - near(other)), device_id_type=MESH
        )
    for step in range(1, SNK):
        pl.semaphore_signal(barrier, inc=1, device_id=ids(s, (y + step) % SNK, m), device_id_type=MESH)
    pl.semaphore_wait(barrier, SRC - 1 + 4 + SNK - 1)

    rows = pl.ds(pl.multiple_of(y * 64, 64), 64)

    def s_step(j):
        source = ek_ref.at[:, :, rows, :] if j == 1 else sbuf.at[j - 1]
        return remote(source, sbuf.at[j], s_send.at[j - 1], s_recv.at[j - 1], onward)

    def e_cross(t):
        return remote(
            es_ref.at[t, pl.ds(2 * y, 2)], ebuf.at[t, pl.ds(8 * m + 2 * y, 2)],
            e_send.at[t], e_recv.at[t], partner,
        )

    def p_wait(t):
        whole = pbuf.at[t, pl.ds(4 * y, 4)]
        return remote(whole, whole, p_send.at[t], p_recv.at[t], up)

    def p_sent(t):
        part_of = per_ref.at[pl.ds(0, SRC - 1)]
        return remote(part_of, part_of, p_send.at[t], p_recv.at[t], up)

    s_step(1).start()
    for t in range(OWN):
        e_cross(t).start()
    for t in range(OWN):
        pltpu.make_async_copy(
            per_ref.at[OWN * s + t],
            pbuf.at[t, pl.ds(4 * y, 4), pl.ds(pl.multiple_of(8 * s, 8), 8)],
            p_recv.at[t],
        ).start()

        def scatter(step, carry, t=t):
            other = (s + step) % SRC
            remote(
                per_ref.at[OWN * other + t],
                pbuf.at[t, pl.ds(4 * y, 4), pl.ds(pl.multiple_of(8 * s, 8), 8)],
                p_send.at[t], p_recv.at[t], ids(other, y, near(other)),
            ).start()
            return carry

        lax.fori_loop(1, SRC, scatter, 0)

    own_e = [
        pltpu.make_async_copy(es_ref.at[t], ebuf.at[t, pl.ds(8 * m, 8)], local_sem.at[t])
        for t in range(OWN)
    ]
    own_s = pltpu.make_async_copy(ek_ref.at[:, :, rows, :], sbuf.at[0], local_sem.at[OWN])
    for copy in own_e + [own_s]:
        copy.start()

    def ring(piece, send, recv, t):
        def copy(which):
            if which < 2:
                source, where = piece(y), (up, down)[which]
            else:
                whole = piece((y + (3, 1)[which - 2]) % SNK)
                count = whole.shape[0] // 2
                source, where = whole.at[pl.ds((which - 2) * count, count)], (up, down)[which - 2]
            return remote(source, source, send.at[t, which], recv.at[t, which], where)

        return copy

    def p_ring(t):
        return ring(lambda row: pbuf.at[t, pl.ds(4 * row, 4)], py_send, py_recv, t)

    def e_ring(t):
        base = 8 * (1 - m)
        return ring(lambda row: ebuf.at[t, pl.ds(base + 2 * row, 2)], ey_send, ey_recv, t)

    def spread(copies):
        copies(0).start()
        copies(1).start()

    def forward(copies):
        copies(0).wait_recv()
        copies(2).start()
        copies(1).wait_recv()
        copies(3).start()

    def s_next(j):
        s_step(j - 1).wait_recv()
        s_step(j).start()

    s_next(2)
    for t in range(OWN):
        p_wait(t).wait_recv()
        spread(p_ring(t))
        e_cross(t).wait_recv()
        spread(e_ring(t))
        s_next(3 + t)
    for t in range(OWN):
        forward(p_ring(t))
        forward(e_ring(t))
    for t in range(OWN):
        for copies in (p_ring(t), e_ring(t)):
            copies(2).wait_recv()
            copies(3).wait_recv()
    s_step(5).wait_recv()
    for copy in own_e + [own_s]:
        copy.wait()

    acc[...] = jnp.zeros_like(acc)
    for t in range(OWN):

        def half(f, carry, t=t):
            mine = pbuf[t, :, rows, :].reshape(16 * 64, 256)
            hbuf[f] = jnp.dot(
                mine, ebuf[t, f], preferred_element_type=f32
            ).astype(jnp.bfloat16).reshape(16, 64, 256)
            return carry

        lax.fori_loop(0, 16, half, 0)

        def pair(ts, carry, t=t):
            at = t + ts
            block = at // OWN
            slot = jnp.where(s % 8 + block >= 8, 1 - m, m)
            sink = sbuf[block, at % OWN].reshape(8 * 64, 256)
            g = jnp.dot(sink, pbuf[t, ts], preferred_element_type=f32).astype(jnp.bfloat16)
            g = g.reshape(8, 64, 256)
            total = acc[slot, ts]
            for a in range(4):
                total += lax.dot_general(
                    g[:, a * 16 : a * 16 + 16].reshape(128, 256),
                    hbuf[:, ts, a * 16 : a * 16 + 16].reshape(256, 256),
                    (((1,), (1,)), ((), ())),
                    preferred_element_type=f32,
                )
            acc[slot, ts] = total
            return carry

        lax.fori_loop(0, 16, pair, 0)

    row = lax.broadcasted_iota(jnp.int32, (128, 256), 0) % 16
    col = lax.broadcasted_iota(jnp.int32, (128, 256), 1) % 16
    keep = row == col

    def fold(i, carry):
        masked = jnp.where(keep, acc[i // 16, i % 16], 0.0)
        full[pl.ds(pl.multiple_of(i * 8, 8), 8)] = masked.reshape(8, 16, 256).sum(axis=1)
        return carry

    lax.fori_loop(0, 32, fold, 0)
    pick = (
        lax.broadcasted_iota(jnp.int32, (16, 256), 1) // 16
        == lax.broadcasted_iota(jnp.int32, (16, 256), 0)
    ).astype(f32)
    mine = lax.dot_general(
        pick, full[...], (((1,), (1,)), ((), ())),
        preferred_element_type=f32, precision=lax.Precision.HIGHEST,
    )

    def gather_sum(value, buffer, count, index, where, stage):
        part[stage] = value
        buffer[index] = value
        for step in range(1, count):
            remote(
                part.at[stage], buffer.at[index], r_send.at[stage], r_recv.at[stage],
                where((index + step) % count),
            ).start()
        most = buffer.at[pl.ds(0, count - 1)]
        done = remote(most, most, r_send.at[stage], r_recv.at[stage], up)
        done.wait_recv()
        done.wait_send()
        total = buffer[0]
        for i in range(1, count):
            total += buffer[i]
        return total

    mine = gather_sum(
        mine, red_a, 8, x * 2 + core,
        lambda i: ids((i // 2) * 8 + zl * 2 + i % 2, y, m), 0,
    )
    mine = gather_sum(
        mine, red_b, 8, m * 4 + zl,
        lambda i: ids(x * 8 + (i % 4) * 2 + core, y, i // 4), 1,
    )
    mine = gather_sum(mine, red_c, 4, y, lambda i: ids(s, i, m), 2)

    mine = mine * norm
    weights = jnp.broadcast_to(hlt_ref[...][None, :, None, :], (2, 16, 8, 128)).reshape(256, 128)
    at = lax.broadcasted_iota(jnp.int32, (256, 128), 0)
    elem = (at // 128) * 8 + at % 8
    for o in range(2):
        chosen = jnp.where(elem == op_ref[2 * s + o], weights, 0.0)
        full[pl.ds(0, 16), pl.ds(0, 128)] = jnp.dot(
            mine, chosen, preferred_element_type=f32, precision=lax.Precision.HIGHEST
        )
        out_ref[o] = full[pl.ds(pl.multiple_of(8 * m, 8), 8), pl.ds(0, 128)]

    for j in range(1, BLOCKS):
        s_step(j).wait_send()
    for t in range(OWN):
        e_cross(t).wait_send()
        for copies in (p_ring(t), e_ring(t)):
            for which in range(4):
                copies(which).wait_send()
        p_sent(t).wait_send()


def body(norm, peramb, elem_src, elem_snk, op_elem, hlt_kernel):
    bf16, f32 = jnp.bfloat16, jnp.float32
    dma = pltpu.SemaphoreType.DMA
    anywhere = pl.BlockSpec(memory_space=pl.ANY)
    return pl.pallas_call(
        functools.partial(kernel, norm),
        out_shape=jax.ShapeDtypeStruct((2, 8, 128), f32),
        in_specs=[
            anywhere, anywhere, anywhere,
            pl.BlockSpec(memory_space=pltpu.SMEM),
            pl.BlockSpec(memory_space=pltpu.VMEM),
        ],
        out_specs=pl.BlockSpec(memory_space=pltpu.VMEM),
        scratch_shapes=[
            pltpu.VMEM((OWN, 16, 256, 256), bf16),
            pltpu.VMEM((OWN, 16, 256, 256), bf16),
            pltpu.VMEM((BLOCKS, OWN, 8, 64, 256), bf16),
            pltpu.VMEM((16, 16, 64, 256), bf16),
            pltpu.VMEM((2, 16, 128, 256), f32),
            pltpu.VMEM((3, 16, 256), f32),
            pltpu.VMEM((8, 16, 256), f32),
            pltpu.VMEM((8, 16, 256), f32),
            pltpu.VMEM((4, 16, 256), f32),
            pltpu.VMEM((256, 256), f32),
            dma((OWN + 1,)), dma((OWN,)), dma((OWN,)), dma((OWN,)), dma((OWN,)),
            dma((BLOCKS - 1,)), dma((BLOCKS - 1,)),
            dma((OWN, 4)), dma((OWN, 4)), dma((OWN, 4)), dma((OWN, 4)),
            dma((3,)), dma((3,)),
        ],
        compiler_params=pltpu.CompilerParams(
            collective_id=0, has_side_effects=True, vmem_limit_bytes=56 * 1024 * 1024
        ),
    )(peramb, elem_src, elem_snk, op_elem, hlt_kernel)


def solution(mesh):
    placed = (
        P(None, "snk", "src", None),
        P("src", "mom", None, None),
        P("src", "mom", None, None),
        P(),
        P(),
    )
    norm = 1.0 / (256 * math.sqrt(96))
    return jax.shard_map(
        functools.partial(body, norm), mesh=mesh, in_specs=placed,
        out_specs=P("src", "mom", None), check_vma=False,
    )
```

time: 999 us -> 209 us (0.21)
  waiting for transfers between devices: 662 us -> 0 us
  Pallas kernels: 0 us -> 207 us
  blocking collectives: 139 us -> 0 us
  starting transfers between devices: 80.2 us -> 0 us
  local copies, waits for them, and re-layouts: 55.6 us -> 1.3 us
  matrix products: 41.5 us -> 0 us
  between operations: 14.1 us -> 0.01 us
    ppermute x5 -> x0, waiting for transfers between devices: 354 us -> none  [shifted(): return lax.ppermute(value, axis, pairs)]
    all_to_all x1 -> x0, waiting for transfers between devices: 307 us -> none  [body(): lax.all_to_all(peramb, 'src', split_axis=0, concat_axis=2, tiled=True)]
    pallas_call x0 -> x1, Pallas kernels: none -> 207 us  [body(): pl.pallas_call(functools.partial(kernel, norm), out_shape=jax.ShapeDtypeS...]
    unnamed x1 -> x0, blocking collectives: 129 us -> none
    all_to_all x1 -> x0, starting transfers between devices: 69.1 us -> none  [body(): lax.all_to_all(peramb, 'src', split_axis=0, concat_axis=2, tiled=True)]
    dot_general x6 -> x0, matrix products: 41.5 us -> none  [the longest x3 29.2 us: body(): jnp.einsum('seab,sfab->sef', block_elems[source_row:source_row + sep_loca...]
    unnamed x21 -> x1, local copies, waits for them, and re-layouts: 20 us -> 1.3 us
    slice x1 -> x0, local copies, waits for them, and re-layouts: 16.6 us -> none  [body(): block_elems[source_row:source_row + sep_local]]
  transfers between devices with their start and end apart: 7 -> 0, of which waited for: 4 -> 0; matrix products, arithmetic and copies ran while one was open for 4% -> 0% of each run, Pallas kernels for 0% -> 0%
where the time goes in v1:
time: 209 us
  Pallas kernels  207 us (99%)
    pallas_call x1, Pallas kernels, body(): pl.pallas_call(functools.partial(kernel, norm), out_shape=jax.ShapeDtypeS...  207 us

profile of v1, /device:TPU:1, one launch (start us, length us, event | category | flops | bytes accessed | tf_op | source)
XLA Modules:
  0.0 208.7 jit_solution(4873941836457030717)
XLA Ops:
  0.0 207.4 %shard_map.55 = f32[2,8,128]{2,1,0:T(8,128)} custom-call(bf16[96,4,8,256]{3,2,1,0:T(8,128)(2,1)} %per_ref.1, bf16[3,8,256,256]{3,2,1,0:T(8,128)(2,1)} %es_ref.1, bf16[3,8,256,256]{3,2,1,0:T(8,128)(2,1)} %ek_ref.1, s32[64]{0:T(128)} %op_ref.1, f32[16,128]{1,0:T(8,128)} %hlt_ref.1), custom_call_target="tpu_custom_call" | custom-call | tf_op jit(solution)/shard_map/pallas_call | solution.py:265
  207.4 1.3 copy.7

commit v2 on v1

--- a/solution.py
+++ b/solution.py
@@ -12,21 +12,26 @@
 SRC, SNK, MOM = 32, 4, 2
 OWN = 3
 BLOCKS = 6
+BRIDGED = (0, 1)
 
 
 def kernel(
     norm, per_ref, es_ref, ek_ref, op_ref, hlt_ref, out_ref,
     pbuf, ebuf, sbuf, hbuf, acc, part, red_a, red_b, red_c, full,
     local_sem, p_send, p_recv, e_send, e_recv, s_send, s_recv,
-    py_send, py_recv, ey_send, ey_recv, r_send, r_recv,
+    py_send, py_recv, ey_send, ey_recv, r_send, r_recv, ebridge, b_send, b_recv,
 ):
     s, y, m = lax.axis_index("src"), lax.axis_index("snk"), lax.axis_index("mom")
     x, zl, core = s // 8, (s // 2) % 4, s % 2
     f32 = jnp.float32
 
-    def near(other):
-        apart = (other // 2) % 4 - zl
-        return jnp.where(apart * apart == 9, 1 - m, m)
+    z = 4 * m + zl
+    lean = 2 - 4 * (z % 2)
+
+    def near(other, sign):
+        apart = ((other // 2) % 4 + 4 - zl) % 4
+        hops = jnp.where(apart == 2, sign * lean, jnp.where(apart == 3, -1, apart))
+        return ((z + 8 + hops) % 8) // 4
 
     def ids(src, snk, mom):
         return {"src": src, "snk": snk, "mom": mom}
@@ -46,14 +51,14 @@
 
     def greet(step, carry):
         other = (s + step) % SRC
-        pl.semaphore_signal(barrier, inc=1, device_id=ids(other, y, near(other)), device_id_type=MESH)
+        pl.semaphore_signal(barrier, inc=1, device_id=ids(other, y, near(other, -1)), device_id_type=MESH)
         return carry
 
     lax.fori_loop(1, SRC, greet, 0)
     for step in range(4):
         other = x * 8 + step * 2 + core
         pl.semaphore_signal(
-            barrier, inc=1, device_id=ids(other, y, 1 - near(other)), device_id_type=MESH
+            barrier, inc=1, device_id=ids(other, y, 1 - near(other, -1)), device_id_type=MESH
         )
     for step in range(1, SNK):
         pl.semaphore_signal(barrier, inc=1, device_id=ids(s, (y + step) % SNK, m), device_id_type=MESH)
@@ -65,10 +70,22 @@
         source = ek_ref.at[:, :, rows, :] if j == 1 else sbuf.at[j - 1]
         return remote(source, sbuf.at[j], s_send.at[j - 1], s_recv.at[j - 1], onward)
 
+    def along_z(hops):
+        to = (z + hops) % 8
+        return ids(x * 8 + (to % 4) * 2 + core, y, to // 4)
+
+    def e_first(t):
+        return remote(
+            es_ref.at[t, pl.ds(2 * y, 2)], ebridge.at[t], b_send.at[t], b_recv.at[t], along_z(2),
+        )
+
     def e_cross(t):
+        if t not in BRIDGED:
+            source, home, where = es_ref.at[t, pl.ds(2 * y, 2)], m, partner
+        else:
+            source, home, where = ebridge.at[t], ((z + 6) % 8) // 4, along_z(2)
         return remote(
-            es_ref.at[t, pl.ds(2 * y, 2)], ebuf.at[t, pl.ds(8 * m + 2 * y, 2)],
-            e_send.at[t], e_recv.at[t], partner,
+            source, ebuf.at[t, pl.ds(8 * home + 2 * y, 2)], e_send.at[t], e_recv.at[t], where,
         )
 
     def p_wait(t):
@@ -79,22 +96,15 @@
         part_of = per_ref.at[pl.ds(0, SRC - 1)]
         return remote(part_of, part_of, p_send.at[t], p_recv.at[t], up)
 
-    s_step(1).start()
-    for t in range(OWN):
-        e_cross(t).start()
-    for t in range(OWN):
-        pltpu.make_async_copy(
-            per_ref.at[OWN * s + t],
-            pbuf.at[t, pl.ds(4 * y, 4), pl.ds(pl.multiple_of(8 * s, 8), 8)],
-            p_recv.at[t],
-        ).start()
-
-        def scatter(step, carry, t=t):
+    def p_scatter(t):
+        where = pbuf.at[t, pl.ds(4 * y, 4), pl.ds(pl.multiple_of(8 * s, 8), 8)]
+        pltpu.make_async_copy(per_ref.at[OWN * s + t], where, p_recv.at[t]).start()
+
+        def scatter(step, carry):
             other = (s + step) % SRC
             remote(
-                per_ref.at[OWN * other + t],
-                pbuf.at[t, pl.ds(4 * y, 4), pl.ds(pl.multiple_of(8 * s, 8), 8)],
-                p_send.at[t], p_recv.at[t], ids(other, y, near(other)),
+                per_ref.at[OWN * other + t], where,
+                p_send.at[t], p_recv.at[t], ids(other, y, near(other, 1)),
             ).start()
             return carry
 
@@ -105,8 +115,13 @@
         for t in range(OWN)
     ]
     own_s = pltpu.make_async_copy(ek_ref.at[:, :, rows, :], sbuf.at[0], local_sem.at[OWN])
-    for copy in own_e + [own_s]:
-        copy.start()
+
+    def e_begin(t):
+        (e_first if t in BRIDGED else e_cross)(t).start()
+
+    def e_bridge(t):
+        e_first(t).wait_recv()
+        e_cross(t).start()
 
     def ring(piece, send, recv, t):
         def copy(which):
@@ -141,37 +156,38 @@
         s_step(j - 1).wait_recv()
         s_step(j).start()
 
-    s_next(2)
-    for t in range(OWN):
+    def p_spread(t):
         p_wait(t).wait_recv()
         spread(p_ring(t))
+
+    def e_spread(t):
         e_cross(t).wait_recv()
         spread(e_ring(t))
-        s_next(3 + t)
-    for t in range(OWN):
+
+    def p_forward(t):
         forward(p_ring(t))
+
+    def e_forward(t):
         forward(e_ring(t))
-    for t in range(OWN):
-        for copies in (p_ring(t), e_ring(t)):
-            copies(2).wait_recv()
-            copies(3).wait_recv()
-    s_step(5).wait_recv()
-    for copy in own_e + [own_s]:
-        copy.wait()
-
-    acc[...] = jnp.zeros_like(acc)
-    for t in range(OWN):
-
-        def half(f, carry, t=t):
-            mine = pbuf[t, :, rows, :].reshape(16 * 64, 256)
-            hbuf[f] = jnp.dot(
+
+    def finish(copies):
+        copies(2).wait_recv()
+        copies(3).wait_recv()
+
+    def halves(t, first):
+        mine = pbuf[t, :, rows, :].reshape(16 * 64, 256)
+
+        def half(i, carry):
+            f = first + i
+            hbuf[t, f] = jnp.dot(
                 mine, ebuf[t, f], preferred_element_type=f32
             ).astype(jnp.bfloat16).reshape(16, 64, 256)
             return carry
 
-        lax.fori_loop(0, 16, half, 0)
-
-        def pair(ts, carry, t=t):
+        lax.fori_loop(0, 8, half, 0, unroll=2)
+
+    def pairs(t, begin, end):
+        def pair(ts, carry):
             at = t + ts
             block = at // OWN
             slot = jnp.where(s % 8 + block >= 8, 1 - m, m)
@@ -182,14 +198,69 @@
             for a in range(4):
                 total += lax.dot_general(
                     g[:, a * 16 : a * 16 + 16].reshape(128, 256),
-                    hbuf[:, ts, a * 16 : a * 16 + 16].reshape(256, 256),
+                    hbuf[t, :, ts, a * 16 : a * 16 + 16].reshape(256, 256),
                     (((1,), (1,)), ((), ())),
                     preferred_element_type=f32,
                 )
             acc[slot, ts] = total
             return carry
 
-        lax.fori_loop(0, 16, pair, 0)
+        lax.fori_loop(begin, end, pair, 0, unroll=2)
+
+    p_scatter(0)
+    s_step(1).start()
+    p_scatter(1)
+    e_begin(0)
+    p_scatter(2)
+    e_begin(1)
+    e_begin(2)
+    own_s.start()
+    own_e[0].start()
+    own_e[1].start()
+    own_e[2].start()
+    acc[...] = jnp.zeros_like(acc)
+    p_spread(0)
+    s_next(2)
+    p_spread(1)
+    e_bridge(0)
+    p_forward(0)
+    p_spread(2)
+    e_bridge(1)
+    s_next(3)
+    e_spread(0)
+    p_forward(1)
+    e_spread(2)
+    e_forward(0)
+    s_next(4)
+    own_s.wait()
+    own_e[0].wait()
+    own_e[1].wait()
+    own_e[2].wait()
+    finish(p_ring(0))
+    halves(0, 8 * m)
+    p_forward(2)
+    e_spread(1)
+    e_forward(2)
+    finish(p_ring(1))
+    halves(1, 8 * m)
+    s_next(5)
+    e_forward(1)
+    finish(e_ring(0))
+    halves(0, 8 - 8 * m)
+    pairs(0, 0, 8)
+    finish(e_ring(2))
+    finish(p_ring(2))
+    halves(2, 8 * m)
+    halves(2, 8 - 8 * m)
+    pairs(0, 8, 14)
+    pairs(2, 0, 12)
+    finish(e_ring(1))
+    halves(1, 8 - 8 * m)
+    pairs(1, 0, 14)
+    s_step(5).wait_recv()
+    pairs(0, 14, 16)
+    pairs(1, 14, 16)
+    pairs(2, 12, 16)
 
     row = lax.broadcasted_iota(jnp.int32, (128, 256), 0) % 16
     col = lax.broadcasted_iota(jnp.int32, (128, 256), 1) % 16
@@ -252,6 +323,8 @@
         s_step(j).wait_send()
     for t in range(OWN):
         e_cross(t).wait_send()
+        if t in BRIDGED:
+            e_first(t).wait_send()
         for copies in (p_ring(t), e_ring(t)):
             for which in range(4):
                 copies(which).wait_send()
@@ -275,7 +348,7 @@
             pltpu.VMEM((OWN, 16, 256, 256), bf16),
             pltpu.VMEM((OWN, 16, 256, 256), bf16),
             pltpu.VMEM((BLOCKS, OWN, 8, 64, 256), bf16),
-            pltpu.VMEM((16, 16, 64, 256), bf16),
+            pltpu.VMEM((OWN, 16, 16, 64, 256), bf16),
             pltpu.VMEM((2, 16, 128, 256), f32),
             pltpu.VMEM((3, 16, 256), f32),
             pltpu.VMEM((8, 16, 256), f32),
@@ -286,6 +359,7 @@
             dma((BLOCKS - 1,)), dma((BLOCKS - 1,)),
             dma((OWN, 4)), dma((OWN, 4)), dma((OWN, 4)), dma((OWN, 4)),
             dma((3,)), dma((3,)),
+            pltpu.VMEM((OWN, 2, 256, 256), bf16), dma((OWN,)), dma((OWN,)),
         ],
         compiler_params=pltpu.CompilerParams(
             collective_id=0, has_side_effects=True, vmem_limit_bytes=56 * 1024 * 1024

time: 209 us -> 154 us (0.74)
  Pallas kernels: 207 us -> 152 us
    pallas_call x1, Pallas kernels: 207 us -> 152 us  [body(): pl.pallas_call(functools.partial(kernel, norm), out_shape=jax.ShapeDtypeS...]
where the time goes in v2:
time: 154 us; the launch traced here: 153 us
  Pallas kernels  152 us (99%)
    pallas_call x1, Pallas kernels, body(): pl.pallas_call(functools.partial(kernel, norm), out_shape=jax.ShapeDtypeS...  152 us

profile of v2, /device:TPU:1, one launch (start us, length us, event | category | flops | bytes accessed | tf_op | source)
XLA Modules:
  0.0 152.9 jit_solution(2142483726661527513)
XLA Ops:
  0.0 151.6 %shard_map.55 = f32[2,8,128]{2,1,0:T(8,128)} custom-call(bf16[96,4,8,256]{3,2,1,0:T(8,128)(2,1)} %per_ref.1, bf16[3,8,256,256]{3,2,1,0:T(8,128)(2,1)} %es_ref.1, bf16[3,8,256,256]{3,2,1,0:T(8,128)(2,1)} %ek_ref.1, s32[64]{0:T(128)} %op_ref.1, f32[16,128]{1,0:T(8,128)} %hlt_ref.1), custom_call_target="tpu_custom_call" | custom-call | tf_op jit(solution)/shard_map/pallas_call | solution.py:338
  151.6 1.3 copy.7

commit v3 on v2

v3 whole, which is shorter than its diff:
```python
import functools
import math

import jax
import jax.numpy as jnp
from jax import lax
from jax.experimental import pallas as pl
from jax.experimental.pallas import tpu as pltpu
from jax.sharding import PartitionSpec as P

MESH = pl.DeviceIdType.MESH
SRC, SNK, MOM = 32, 4, 2
OWN = 3
BLOCKS = 6


def kernel(
    norm, per_ref, es_ref, ek_ref, op_ref, hlt_ref, out_ref,
    pbuf, ebuf, sbuf, hbuf, acc, part, red_a, red_b, red_c, full,
    local_sem, p_send, p_recv, e_send, e_recv, s_send, s_recv,
    py_send, py_recv, ey_send, ey_recv, r_send, r_recv, gbuf, stage_a, stage_c,
):
    s, y, m = lax.axis_index("src"), lax.axis_index("snk"), lax.axis_index("mom")
    x, zl, core = s // 8, (s // 2) % 4, s % 2
    f32 = jnp.float32

    z = 4 * m + zl
    lean = 2

    def near(other, sign):
        apart = ((other // 2) % 4 + 4 - zl) % 4
        hops = jnp.where(apart == 2, sign * lean, jnp.where(apart == 3, -1, apart))
        return ((z + 8 + hops) % 8) // 4

    def ids(src, snk, mom):
        return {"src": src, "snk": snk, "mom": mom}

    def remote(src, dst, send, recv, where):
        return pltpu.make_async_remote_copy(
            src_ref=src, dst_ref=dst, send_sem=send, recv_sem=recv,
            device_id=where, device_id_type=MESH,
        )

    up = ids(s, (y + 1) % SNK, m)
    down = ids(s, (y + 3) % SNK, m)
    partner = ids(s, y, 1 - m)
    onward = ids((s + SRC - 1) % SRC, y, jnp.where(s % 8 == 0, 1 - m, m))

    barrier = pltpu.get_barrier_semaphore()

    def greet(step, carry):
        other = (s + step) % SRC
        pl.semaphore_signal(barrier, inc=1, device_id=ids(other, y, near(other, -1)), device_id_type=MESH)
        return carry

    lax.fori_loop(1, SRC, greet, 0)
    for step in range(4):
        other = x * 8 + step * 2 + core
        pl.semaphore_signal(
            barrier, inc=1, device_id=ids(other, y, 1 - near(other, -1)), device_id_type=MESH
        )
    for step in range(1, SNK):
        pl.semaphore_signal(barrier, inc=1, device_id=ids(s, (y + step) % SNK, m), device_id_type=MESH)
    rows = pl.ds(pl.multiple_of(y * 64, 64), 64)
    own_e = [
        pltpu.make_async_copy(es_ref.at[t], ebuf.at[t, pl.ds(8 * m, 8)], local_sem.at[t])
        for t in range(OWN)
    ]
    own_s = pltpu.make_async_copy(ek_ref.at[:, :, rows, :], sbuf.at[0], local_sem.at[OWN])
    for copy in own_e + [own_s]:
        copy.start()
    acc[...] = jnp.zeros_like(acc)
    pl.semaphore_wait(barrier, SRC - 1 + 4 + SNK - 1)

    def s_step(j):
        source = ek_ref.at[:, :, rows, :] if j == 1 else sbuf.at[j - 1]
        return remote(source, sbuf.at[j], s_send.at[j - 1], s_recv.at[j - 1], onward)

    def s_last():
        above = (z + 1) % 8
        return remote(
            ek_ref.at[:, :, rows, :], sbuf.at[5], s_send.at[4], s_recv.at[4],
            ids((s + SRC - 5) % SRC, y, above // 4),
        )

    def s_early():
        @pl.when(core == 0)
        def _():
            s_last().start()

    def s_late():
        s_step(4).wait_recv()

        @pl.when(core == 1)
        def _():
            s_step(5).start()

    def e_cross(t):
        return remote(
            es_ref.at[t, pl.ds(2 * y, 2)], ebuf.at[t, pl.ds(8 * m + 2 * y, 2)],
            e_send.at[t], e_recv.at[t], partner,
        )

    def p_wait(t):
        whole = pbuf.at[t, pl.ds(4 * y, 4)]
        return remote(whole, whole, p_send.at[t], p_recv.at[t], up)

    def p_sent(t):
        part_of = per_ref.at[pl.ds(0, SRC - 1)]
        return remote(part_of, part_of, p_send.at[t], p_recv.at[t], up)

    def p_scatter(t):
        where = pbuf.at[t, pl.ds(4 * y, 4), pl.ds(pl.multiple_of(8 * s, 8), 8)]
        pltpu.make_async_copy(per_ref.at[OWN * s + t], where, p_recv.at[t]).start()

        def scatter(step, carry):
            other = (s + step) % SRC
            remote(
                per_ref.at[OWN * other + t], where,
                p_send.at[t], p_recv.at[t], ids(other, y, near(other, 1)),
            ).start()
            return carry

        lax.fori_loop(1, SRC, scatter, 0)


    def e_begin(t):
        e_cross(t).start()

    def ring(piece, send, recv, t):
        def copy(which):
            if which < 2:
                source, where = piece(y), (up, down)[which]
            else:
                whole = piece((y + (3, 1)[which - 2]) % SNK)
                count = whole.shape[0] // 2
                source, where = whole.at[pl.ds((which - 2) * count, count)], (up, down)[which - 2]
            return remote(source, source, send.at[t, which], recv.at[t, which], where)

        return copy

    def p_ring(t):
        return ring(lambda row: pbuf.at[t, pl.ds(4 * row, 4)], py_send, py_recv, t)

    def e_ring(t):
        base = 8 * (1 - m)
        return ring(lambda row: ebuf.at[t, pl.ds(base + 2 * row, 2)], ey_send, ey_recv, t)

    def spread(copies):
        copies(0).start()
        copies(1).start()

    def forward(copies):
        copies(0).wait_recv()
        copies(2).start()
        copies(1).wait_recv()
        copies(3).start()

    def s_next(j):
        s_step(j - 1).wait_recv()
        s_step(j).start()

    def p_spread(t):
        p_wait(t).wait_recv()
        spread(p_ring(t))

    def e_spread(t):
        e_cross(t).wait_recv()
        spread(e_ring(t))

    def p_forward(t):
        forward(p_ring(t))

    def e_forward(t):
        forward(e_ring(t))

    def finish(copies):
        copies(2).wait_recv()
        copies(3).wait_recv()

    def halves(t, half):
        mine = pbuf[t, :, rows, :].reshape(16 * 64, 256)

        def one(i, carry):
            hbuf[t, i] = jnp.dot(
                mine, ebuf[t, 8 * half + i], preferred_element_type=f32
            ).astype(jnp.bfloat16).reshape(16, 64, 256)
            return carry

        lax.fori_loop(0, 8, one, 0, unroll=4)

    def traces(t, half, begin, end, fresh, unroll=4):
        def pair(ts, carry):
            at = t + ts
            block = at // OWN
            wraps = (s % 8 + block) // 8
            wraps = jnp.where((block == 5) & (core == 1), 1 - wraps, wraps)
            slot = (m + wraps) % 2
            if fresh:
                sink = sbuf[block, at % OWN].reshape(8 * 64, 256)
                g = jnp.dot(sink, pbuf[t, ts], preferred_element_type=f32).astype(jnp.bfloat16)
                g = g.reshape(8, 64, 256)
                gbuf[t, ts] = g
            else:
                g = gbuf[t, ts]
            total = acc[slot, half, ts]
            for a in range(4):
                total += lax.dot_general(
                    g[:, a * 16 : a * 16 + 16].reshape(128, 256),
                    hbuf[t, :, ts, a * 16 : a * 16 + 16].reshape(128, 256),
                    (((1,), (1,)), ((), ())),
                    preferred_element_type=f32,
                )
            acc[slot, half, ts] = total
            return carry

        lax.fori_loop(begin, end, pair, 0, unroll=min(unroll, end - begin))

    def own_traces(t, begin, end):
        traces(t, m, begin, end, True)

    def other_traces(t):
        halves(t, 1 - m)
        traces(t, 1 - m, 0, 16, False)

    p_scatter(0)
    p_scatter(1)
    p_scatter(2)
    e_begin(0)
    s_step(1).start()
    s_early()
    e_begin(1)
    e_begin(2)
    p_spread(0)
    p_spread(1)
    p_spread(2)
    own_s.wait()
    own_e[0].wait()
    own_e[1].wait()
    own_e[2].wait()
    s_next(2)
    p_forward(0)
    e_spread(0)
    s_next(3)
    p_forward(1)
    e_spread(1)
    s_next(4)
    e_forward(0)
    p_forward(2)
    s_late()
    finish(p_ring(0))
    halves(0, m)
    own_traces(0, 0, 12)
    e_spread(2)
    e_forward(1)
    finish(p_ring(1))
    halves(1, m)
    own_traces(1, 0, 12)
    e_forward(2)
    finish(p_ring(2))
    halves(2, m)
    own_traces(2, 0, 12)
    s_step(5).wait_recv()
    own_traces(0, 12, 16)
    own_traces(1, 12, 16)
    own_traces(2, 12, 16)
    finish(e_ring(0))
    other_traces(0)
    finish(e_ring(1))
    other_traces(1)
    finish(e_ring(2))
    other_traces(2)

    row = lax.broadcasted_iota(jnp.int32, (128, 128), 0) % 16
    col = lax.broadcasted_iota(jnp.int32, (128, 128), 1) % 16
    keep = row == col
    for half in range(2):

        def fold(i, carry, half=half):
            masked = jnp.where(keep, acc[i // 16, half, i % 16], 0.0)
            full[pl.ds(pl.multiple_of(i * 8, 8), 8), half * 128 : half * 128 + 128] = (
                masked.reshape(8, 16, 128).sum(axis=1)
            )
            return carry

        lax.fori_loop(0, 32, fold, 0, unroll=4)
    pick = (
        lax.broadcasted_iota(jnp.int32, (16, 256), 1) // 16
        == lax.broadcasted_iota(jnp.int32, (16, 256), 0)
    ).astype(f32)
    mine = lax.dot_general(
        pick, full[...], (((1,), (1,)), ((), ())),
        preferred_element_type=f32, precision=lax.Precision.HIGHEST,
    )

    part[...] = mine

    def gather_sum(source, held, buffer, count, index, where, stage):
        buffer[index] = held
        for step in range(1, count):
            to = (index + step) % count
            remote(
                source(to), buffer.at[index], r_send.at[stage], r_recv.at[stage], where(to),
            ).start()
        most = buffer.at[pl.ds(0, count - 1)]
        done = remote(most, most, r_send.at[stage], r_recv.at[stage], up)
        done.wait_recv()
        total = buffer[0]
        for i in range(1, count):
            total += buffer[i]
        return total

    def rows_of(half):
        return pl.ds(pl.multiple_of(8 * half, 8), 8)

    mine = gather_sum(
        lambda i: part.at[rows_of(i // 4)], part[rows_of(m)], red_b, 8, z,
        lambda i: ids(x * 8 + (i % 4) * 2 + core, y, i // 4), 0,
    )
    stage_a[...] = mine
    mine = gather_sum(
        lambda i: stage_a, mine, red_a, 8, x * 2 + core,
        lambda i: ids((i // 2) * 8 + zl * 2 + i % 2, y, m), 1,
    )
    stage_c[...] = mine
    mine = gather_sum(lambda i: stage_c, mine, red_c, 4, y, lambda i: ids(s, i, m), 2)

    mine = mine * norm
    weights = jnp.broadcast_to(hlt_ref[...][None, :, None, :], (2, 16, 8, 128)).reshape(256, 128)
    at = lax.broadcasted_iota(jnp.int32, (256, 128), 0)
    elem = (at // 128) * 8 + at % 8
    for o in range(2):
        chosen = jnp.where(elem == op_ref[2 * s + o], weights, 0.0)
        out_ref[o] = jnp.dot(
            mine, chosen, preferred_element_type=f32, precision=lax.Precision.HIGHEST
        )

    for buffer, count, stage in ((red_b, 8, 0), (red_a, 8, 1), (red_c, 4, 2)):
        most = buffer.at[pl.ds(0, count - 1)]
        remote(most, most, r_send.at[stage], r_recv.at[stage], up).wait_send()
    for j in range(1, BLOCKS):
        s_step(j).wait_send()
    for t in range(OWN):
        e_cross(t).wait_send()
        for copies in (p_ring(t), e_ring(t)):
            for which in range(4):
                copies(which).wait_send()
        p_sent(t).wait_send()


def body(norm, peramb, elem_src, elem_snk, op_elem, hlt_kernel):
    bf16, f32 = jnp.bfloat16, jnp.float32
    dma = pltpu.SemaphoreType.DMA
    anywhere = pl.BlockSpec(memory_space=pl.ANY)
    return pl.pallas_call(
        functools.partial(kernel, norm),
        out_shape=jax.ShapeDtypeStruct((2, 8, 128), f32),
        in_specs=[
            anywhere, anywhere, anywhere,
            pl.BlockSpec(memory_space=pltpu.SMEM),
            pl.BlockSpec(memory_space=pltpu.VMEM),
        ],
        out_specs=pl.BlockSpec(memory_space=pltpu.VMEM),
        scratch_shapes=[
            pltpu.VMEM((OWN, 16, 256, 256), bf16),
            pltpu.VMEM((OWN, 16, 256, 256), bf16),
            pltpu.VMEM((BLOCKS, OWN, 8, 64, 256), bf16),
            pltpu.VMEM((OWN, 8, 16, 64, 256), bf16),
            pltpu.VMEM((2, 2, 16, 128, 128), f32),
            pltpu.VMEM((16, 256), f32),
            pltpu.VMEM((8, 8, 256), f32),
            pltpu.VMEM((8, 8, 256), f32),
            pltpu.VMEM((4, 8, 256), f32),
            pltpu.VMEM((256, 256), f32),
            dma((OWN + 1,)), dma((OWN,)), dma((OWN,)), dma((OWN,)), dma((OWN,)),
            dma((BLOCKS - 1,)), dma((BLOCKS - 1,)),
            dma((OWN, 4)), dma((OWN, 4)), dma((OWN, 4)), dma((OWN, 4)),
            dma((3,)), dma((3,)),
            pltpu.VMEM((OWN, 16, 8, 64, 256), bf16),
            pltpu.VMEM((8, 256), f32), pltpu.VMEM((8, 256), f32),
        ],
        compiler_params=pltpu.CompilerParams(
            collective_id=0, has_side_effects=True, vmem_limit_bytes=56 * 1024 * 1024
        ),
    )(peramb, elem_src, elem_snk, op_elem, hlt_kernel)


def solution(mesh):
    placed = (
        P(None, "snk", "src", None),
        P("src", "mom", None, None),
        P("src", "mom", None, None),
        P(),
        P(),
    )
    norm = 1.0 / (256 * math.sqrt(96))
    return jax.shard_map(
        functools.partial(body, norm), mesh=mesh, in_specs=placed,
        out_specs=P("src", "mom", None), check_vma=False,
    )
```

time: 154 us -> 133 us (0.86)
  Pallas kernels: 152 us -> 132 us
    pallas_call x1, Pallas kernels: 152 us -> 132 us  [body(): pl.pallas_call(functools.partial(kernel, norm), out_shape=jax.ShapeDtypeS...]
where the time goes in v3:
time: 133 us
  Pallas kernels  132 us (99%)
    pallas_call x1, Pallas kernels, body(): pl.pallas_call(functools.partial(kernel, norm), out_shape=jax.ShapeDtypeS...  132 us

profile of v3, /device:TPU:1, one launch (start us, length us, event | category | flops | bytes accessed | tf_op | source)
XLA Modules:
  0.0 133.2 jit_solution(12168584988501938729)
XLA Ops:
  0.0 131.9 %shard_map.55 = f32[2,8,128]{2,1,0:T(8,128)} custom-call(bf16[96,4,8,256]{3,2,1,0:T(8,128)(2,1)} %per_ref.1, bf16[3,8,256,256]{3,2,1,0:T(8,128)(2,1)} %es_ref.1, bf16[3,8,256,256]{3,2,1,0:T(8,128)(2,1)} %ek_ref.1, s32[64]{0:T(128)} %op_ref.1, f32[16,128]{1,0:T(8,128)} %hlt_ref.1), custom_call_target="tpu_custom_call" | custom-call | tf_op jit(solution)/shard_map/pallas_call | solution.py:355
  132.0 1.3 copy.7

commit v4 on v3

--- a/solution.py
+++ b/solution.py
@@ -129,13 +129,13 @@
 
     def ring(piece, send, recv, t):
         def copy(which):
-            if which < 2:
-                source, where = piece(y), (up, down)[which]
-            else:
-                whole = piece((y + (3, 1)[which - 2]) % SNK)
-                count = whole.shape[0] // 2
-                source, where = whole.at[pl.ds((which - 2) * count, count)], (up, down)[which - 2]
-            return remote(source, source, send.at[t, which], recv.at[t, which], where)
+            back = which % 2
+            row = y if which < 4 else (y + (3, 1)[back]) % SNK
+            whole = piece(row)
+            count = whole.shape[0] // 2
+            later = which in (1, 2, 5)
+            source = whole.at[pl.ds(later * count, count)]
+            return remote(source, source, send.at[t, which], recv.at[t, which], (up, down)[back])
 
         return copy
 
@@ -147,14 +147,14 @@
         return ring(lambda row: ebuf.at[t, pl.ds(base + 2 * row, 2)], ey_send, ey_recv, t)
 
     def spread(copies):
-        copies(0).start()
-        copies(1).start()
+        for which in range(4):
+            copies(which).start()
 
     def forward(copies):
         copies(0).wait_recv()
-        copies(2).start()
+        copies(4).start()
         copies(1).wait_recv()
-        copies(3).start()
+        copies(5).start()
 
     def s_next(j):
         s_step(j - 1).wait_recv()
@@ -175,8 +175,8 @@
         forward(e_ring(t))
 
     def finish(copies):
-        copies(2).wait_recv()
-        copies(3).wait_recv()
+        for which in range(2, 6):
+            copies(which).wait_recv()
 
     def halves(t, half):
         mine = pbuf[t, :, rows, :].reshape(16 * 64, 256)
@@ -240,25 +240,25 @@
     own_e[2].wait()
     s_next(2)
     p_forward(0)
+    p_forward(1)
+    s_next(3)
     e_spread(0)
-    s_next(3)
-    p_forward(1)
-    e_spread(1)
+    p_forward(2)
     s_next(4)
-    e_forward(0)
-    p_forward(2)
-    s_late()
     finish(p_ring(0))
     halves(0, m)
+    e_spread(1)
+    e_forward(0)
     own_traces(0, 0, 12)
+    s_late()
     e_spread(2)
-    e_forward(1)
     finish(p_ring(1))
     halves(1, m)
+    e_forward(1)
     own_traces(1, 0, 12)
-    e_forward(2)
     finish(p_ring(2))
     halves(2, m)
+    e_forward(2)
     own_traces(2, 0, 12)
     s_step(5).wait_recv()
     own_traces(0, 12, 16)
@@ -343,7 +343,7 @@
     for t in range(OWN):
         e_cross(t).wait_send()
         for copies in (p_ring(t), e_ring(t)):
-            for which in range(4):
+            for which in range(6):
                 copies(which).wait_send()
         p_sent(t).wait_send()
 
@@ -374,7 +374,7 @@
             pltpu.VMEM((256, 256), f32),
             dma((OWN + 1,)), dma((OWN,)), dma((OWN,)), dma((OWN,)), dma((OWN,)),
             dma((BLOCKS - 1,)), dma((BLOCKS - 1,)),
-            dma((OWN, 4)), dma((OWN, 4)), dma((OWN, 4)), dma((OWN, 4)),
+            dma((OWN, 6)), dma((OWN, 6)), dma((OWN, 6)), dma((OWN, 6)),
             dma((3,)), dma((3,)),
             pltpu.VMEM((OWN, 16, 8, 64, 256), bf16),
             pltpu.VMEM((8, 256), f32), pltpu.VMEM((8, 256), f32),

time: 133 us -> 128 us (0.962)
  Pallas kernels: 132 us -> 126 us
    pallas_call x1, Pallas kernels: 132 us -> 126 us  [body(): pl.pallas_call(functools.partial(kernel, norm), out_shape=jax.ShapeDtypeS...]
where the time goes in v4:
time: 128 us
  Pallas kernels  126 us (98%)
  local copies, waits for them, and re-layouts  1.3 us (1%)
    pallas_call x1, Pallas kernels, body(): pl.pallas_call(functools.partial(kernel, norm), out_shape=jax.ShapeDtypeS...  126 us

profile of v4, /device:TPU:1, one launch (start us, length us, event | category | flops | bytes accessed | tf_op | source)
XLA Modules:
  0.0 127.8 jit_solution(8987733923697506114)
XLA Ops:
  0.0 126.4 %shard_map.55 = f32[2,8,128]{2,1,0:T(8,128)} custom-call(bf16[96,4,8,256]{3,2,1,0:T(8,128)(2,1)} %per_ref.1, bf16[3,8,256,256]{3,2,1,0:T(8,128)(2,1)} %es_ref.1, bf16[3,8,256,256]{3,2,1,0:T(8,128)(2,1)} %ek_ref.1, s32[64]{0:T(128)} %op_ref.1, f32[16,128]{1,0:T(8,128)} %hlt_ref.1), custom_call_target="tpu_custom_call" | custom-call | tf_op jit(solution)/shard_map/pallas_call | solution.py:355
  126.5 1.3 %copy.7 = f32[2,8,128]{2,1,0:T(8,128)} copy(f32[2,8,128]{2,1,0:T(8,128)} %shard_map.55) | data formatting | bytes 16384

commit v5 on v4

--- a/solution.py
+++ b/solution.py
@@ -187,9 +187,9 @@
             ).astype(jnp.bfloat16).reshape(16, 64, 256)
             return carry
 
-        lax.fori_loop(0, 8, one, 0, unroll=4)
-
-    def traces(t, half, begin, end, fresh, unroll=4):
+        lax.fori_loop(0, 8, one, 0, unroll=8)
+
+    def traces(t, half, begin, end, fresh, unroll=12):
         def pair(ts, carry):
             at = t + ts
             block = at // OWN
@@ -221,7 +221,7 @@
 
     def other_traces(t):
         halves(t, 1 - m)
-        traces(t, 1 - m, 0, 16, False)
+        traces(t, 1 - m, 0, 16, False, 16)
 
     p_scatter(0)
     p_scatter(1)

time: 128 us -> 125 us (0.977)
  Pallas kernels: 126 us -> 123 us
    pallas_call x1, Pallas kernels: 126 us -> 123 us  [body(): pl.pallas_call(functools.partial(kernel, norm), out_shape=jax.ShapeDtypeS...]
where the time goes in v5:
time: 125 us; the launch traced here: 124 us
  Pallas kernels  123 us (98%)
  local copies, waits for them, and re-layouts  1.3 us (1%)
    pallas_call x1, Pallas kernels, body(): pl.pallas_call(functools.partial(kernel, norm), out_shape=jax.ShapeDtypeS...  123 us

profile of v5, /device:TPU:1, one launch (start us, length us, event | category | flops | bytes accessed | tf_op | source)
XLA Modules:
  0.0 124.5 jit_solution(5583557019430037367)
XLA Ops:
  0.0 123.2 %shard_map.55 = f32[2,8,128]{2,1,0:T(8,128)} custom-call(bf16[96,4,8,256]{3,2,1,0:T(8,128)(2,1)} %per_ref.1, bf16[3,8,256,256]{3,2,1,0:T(8,128)(2,1)} %es_ref.1, bf16[3,8,256,256]{3,2,1,0:T(8,128)(2,1)} %ek_ref.1, s32[64]{0:T(128)} %op_ref.1, f32[16,128]{1,0:T(8,128)} %hlt_ref.1), custom_call_target="tpu_custom_call" | custom-call | tf_op jit(solution)/shard_map/pallas_call | solution.py:355
  123.2 1.3 %copy.7 = f32[2,8,128]{2,1,0:T(8,128)} copy(f32[2,8,128]{2,1,0:T(8,128)} %shard_map.55) | data formatting | bytes 16384

commit v6 on v5

--- a/solution.py
+++ b/solution.py
@@ -189,7 +189,7 @@
 
         lax.fori_loop(0, 8, one, 0, unroll=8)
 
-    def traces(t, half, begin, end, fresh, unroll=12):
+    def traces(t, half, begin, end, fresh, unroll=16):
         def pair(ts, carry):
             at = t + ts
             block = at // OWN
@@ -259,11 +259,10 @@
     finish(p_ring(2))
     halves(2, m)
     e_forward(2)
-    own_traces(2, 0, 12)
     s_step(5).wait_recv()
+    own_traces(2, 0, 16)
     own_traces(0, 12, 16)
     own_traces(1, 12, 16)
-    own_traces(2, 12, 16)
     finish(e_ring(0))
     other_traces(0)
     finish(e_ring(1))
@@ -283,7 +282,7 @@
             )
             return carry
 
-        lax.fori_loop(0, 32, fold, 0, unroll=4)
+        lax.fori_loop(0, 32, fold, 0, unroll=8)
     pick = (
         lax.broadcasted_iota(jnp.int32, (16, 256), 1) // 16
         == lax.broadcasted_iota(jnp.int32, (16, 256), 0)

time: 125 us -> 124 us (level)
  no operation moved by 1% of the time
where the time goes in v6:
time: 124 us
  Pallas kernels  123 us (99%)
  local copies, waits for them, and re-layouts  1.3 us (1%)
    pallas_call x1, Pallas kernels, body(): pl.pallas_call(functools.partial(kernel, norm), out_shape=jax.ShapeDtypeS...  123 us

profile of v6, /device:TPU:1, one launch (start us, length us, event | category | flops | bytes accessed | tf_op | source)
XLA Modules:
  0.0 124.0 jit_solution(6587077307599273909)
XLA Ops:
  0.0 122.7 %shard_map.55 = f32[2,8,128]{2,1,0:T(8,128)} custom-call(bf16[96,4,8,256]{3,2,1,0:T(8,128)(2,1)} %per_ref.1, bf16[3,8,256,256]{3,2,1,0:T(8,128)(2,1)} %es_ref.1, bf16[3,8,256,256]{3,2,1,0:T(8,128)(2,1)} %ek_ref.1, s32[64]{0:T(128)} %op_ref.1, f32[16,128]{1,0:T(8,128)} %hlt_ref.1), custom_call_target="tpu_custom_call" | custom-call | tf_op jit(solution)/shard_map/pallas_call | solution.py:354
  122.7 1.3 %copy.7 = f32[2,8,128]{2,1,0:T(8,128)} copy(f32[2,8,128]{2,1,0:T(8,128)} %shard_map.55) | data formatting | bytes 16384
